TPU v7x, 32 devices: a whole 2x2x4 slice. The times are simulated.
32 devices in a mesh: grp: 4 (over x, core), ctx: 4 (over z), wt: 2 (over y).
Axes of the slice: x: 2, y: 2, z: 4, core: 2. Of those that a mesh axis runs over, the one named last changes fastest.
Arguments:
- tokens: bfloat16 [8, 2048, 1280], P(('grp', 'wt'), 'ctx'), may hold values from -6 to 6
- segments: int32 [8, 2048], P(('grp', 'wt')), may hold values from 0 to 2, as said below
- w_qkv: bfloat16 [1280, 3840], P('wt'), may hold values from -0.15625 to 0.15625
- w_proj: bfloat16 [1280, 1280], P('wt'), may hold values from -1.25 to 1.25
- w_in: bfloat16 [1280, 1280], P('wt'), may hold values from -0.15625 to 0.15625
- w_out: bfloat16 [1280, 1280], P('wt'), may hold values from -0.15625 to 0.15625
- gain_attn: float32 [1280], replicated, may hold values from 0.5 to 1.5
- gain_mlp: float32 [1280], replicated, may hold values from 0.5 to 1.5
- query_scale: float32 [80], replicated, may hold values from -0.5 to 1.5
- cotangent: bfloat16 [8, 2048, 1280], P(('grp', 'wt'), 'ctx'), may hold values from -6 to 6
Outputs:
- layer_out: bfloat16 [8, 2048, 1280], P(('grp', 'wt'), 'ctx')
- grad_tokens: bfloat16 [8, 2048, 1280], P(('grp', 'wt'), 'ctx')
- grad_w_qkv: float32 [1280, 3840], P('wt')
- grad_w_proj: float32 [1280, 1280], P('wt')
- grad_w_in: float32 [1280, 1280], P('wt')
- grad_w_out: float32 [1280, 1280], P('wt')
- grad_gain_attn: float32 [1280], replicated
- grad_gain_mlp: float32 [1280], replicated
- grad_query_scale: float32 [80], replicated
Inputs may be any that keep to these rules, and one draw needn't show every extreme that they name: `segments`: in each group the id starts at 0, never falls, and every id of 0 to 2 is used. Segment 0 ends 1024 - r tokens into the group, r below 256; each later continuation starts 512 + j tokens after the one before, j within 128 either way; the last runs to the group's end.
All inputs are finite; a program needn't handle non-finite values.
Results may differ from a plain program's by a relative error of at most 0.02.
Values may be sent and summed in bfloat16 or wider, within the bound.
No kernel may reach another device: no remote copies, remote signals or barrier semaphores. Data moves between devices by JAX's collectives and lax.ppermute only.
A program may use at most 256 MiB of HBM per device.

v0:
```python
import math
import jax
import jax.numpy as jnp
from jax import lax
from jax.sharding import PartitionSpec as P

D = 1280
H = 16
HD = 80
epsilon = 1e-06
scale_base = 1.442695041
masked_fill = -1e30


def rms_inverse(values):
    return lax.rsqrt(jnp.mean(values * values, axis=-1, keepdims=True) + epsilon)


def norm_back(values, inverse, grad_scaled):
    return inverse * grad_scaled - values * (inverse * inverse * inverse) * jnp.mean(
        grad_scaled * values, axis=-1, keepdims=True
    )


def times_trans(left, right):
    return lax.dot_general(
        left, right, (((1,), (1,)), ((), ())), preferred_element_type=jnp.float32
    )


def trans_times(left, right):
    return lax.dot_general(
        left, right, (((0,), (0,)), ((), ())), preferred_element_type=jnp.float32
    )


def visible(query_pos, query_seg, seg_row, offset, key_count):
    key_pos = offset + jnp.arange(key_count, dtype=jnp.int32)
    key_seg = lax.dynamic_slice_in_dim(seg_row, offset, key_count)
    return (key_pos[None, :] <= query_pos[:, None]) & (
        (key_seg[None, :] == 0) | (key_seg[None, :] == query_seg[:, None])
    )


def blocked(step_fn, carried, shard_rows):
    length = shard_rows.shape[0]
    width = math.gcd(length, 512)

    def advance(counter, carried_in):
        beginning = counter * width
        subrows = lax.dynamic_slice_in_dim(shard_rows, beginning, width, 0)
        return step_fn(carried_in, subrows, beginning)

    return lax.fori_loop(0, length // width, advance, carried)


def local(
    tokens, segments, w_qkv, w_proj, w_in, w_out, gain_attn, gain_mlp, query_scale, cotangent
):
    inputs = tokens[0].astype(jnp.float32)
    rows = inputs.shape[0]
    seg_row = segments[0]
    group_len = seg_row.shape[0]
    own_index = lax.axis_index("ctx")
    own_offset = own_index * rows
    query_pos = own_offset + jnp.arange(rows, dtype=jnp.int32)
    query_seg = lax.dynamic_slice_in_dim(seg_row, own_offset, rows)
    full_qkv, full_proj, full_in, full_out = (
        lax.all_gather(w_qkv, "wt", axis=0, tiled=True),
        lax.all_gather(w_proj, "wt", axis=0, tiled=True),
        lax.all_gather(w_in, "wt", axis=0, tiled=True),
        lax.all_gather(w_out, "wt", axis=0, tiled=True),
    )
    inverse_attn = rms_inverse(inputs)
    normed = (inputs * inverse_attn * gain_attn).astype(jnp.bfloat16)
    project = jnp.dot(normed, full_qkv, preferred_element_type=jnp.float32)
    dim_scale = scale_base / math.sqrt(HD) * jax.nn.softplus(query_scale)
    raw_queries = project[:, :D].reshape(rows, H, HD)
    queries = (raw_queries * dim_scale).astype(jnp.bfloat16)
    keyval = project[:, D:].astype(jnp.bfloat16)

    def forward_step(carried, subrows, offset):
        running_max, running_sum, accum = carried
        key_count = subrows.shape[0]
        keys_part = subrows[:, :D].reshape(key_count, H, HD)
        values_part = subrows[:, D:].reshape(key_count, H, HD)
        scores = jnp.einsum("qhd,khd->hqk", queries, keys_part, preferred_element_type=jnp.float32)
        allowed = visible(query_pos, query_seg, seg_row, offset, key_count)[None]
        masked = jnp.where(allowed, scores, masked_fill)
        new_max = jnp.maximum(running_max, jnp.max(masked, axis=-1))
        factor = jnp.exp(running_max - new_max)
        exponent = jnp.where(allowed, jnp.exp(masked - new_max[:, :, None]), 0.0)
        running_sum = running_sum * factor + jnp.sum(exponent, axis=-1)
        accum = accum * jnp.transpose(factor)[:, :, None] + jnp.einsum(
            "hqk,khd->qhd",
            exponent.astype(jnp.bfloat16),
            values_part,
            preferred_element_type=jnp.float32,
        )
        return (new_max, running_sum, accum)

    start_state = (
        jnp.full((H, rows), masked_fill, jnp.float32),
        jnp.zeros((H, rows), jnp.float32),
        jnp.zeros((rows, H, HD), jnp.float32),
    )
    running_max, running_sum, accum = blocked(
        forward_step, start_state, lax.all_gather(keyval, "ctx", axis=0, tiled=True)
    )
    logsum = running_max + jnp.log(running_sum)
    attn_float = accum / jnp.transpose(running_sum)[:, :, None]
    attended = attn_float.reshape(rows, D).astype(jnp.bfloat16)
    resid = inputs + jnp.dot(attended, full_proj, preferred_element_type=jnp.float32)
    inverse_mlp = rms_inverse(resid)
    normed_mlp = (resid * inverse_mlp * gain_mlp).astype(jnp.bfloat16)
    hidden = jnp.dot(normed_mlp, full_in, preferred_element_type=jnp.float32)
    active = jax.nn.silu(hidden).astype(jnp.bfloat16)
    layer_out = (resid + jnp.dot(active, full_out, preferred_element_type=jnp.float32)).astype(
        jnp.bfloat16
    )
    back_qkv, back_proj, back_in, back_out = (
        lax.all_gather(w_qkv, "wt", axis=0, tiled=True),
        lax.all_gather(w_proj, "wt", axis=0, tiled=True),
        lax.all_gather(w_in, "wt", axis=0, tiled=True),
        lax.all_gather(w_out, "wt", axis=0, tiled=True),
    )
    grad_out = cotangent[0].astype(jnp.float32)
    grad_mlp = cotangent[0]
    grad_active = times_trans(grad_mlp, back_out)
    grad_w_out = trans_times(active, grad_mlp)
    sigmoid_h = jax.nn.sigmoid(hidden)
    grad_hidden = (grad_active * sigmoid_h * (1.0 + hidden * (1.0 - sigmoid_h))).astype(
        jnp.bfloat16
    )
    grad_w_in = trans_times(normed_mlp, grad_hidden)
    grad_normed_mlp = times_trans(grad_hidden, back_in)
    grad_gain_mlp = jnp.sum(grad_normed_mlp * resid * inverse_mlp, axis=0)
    grad_resid = grad_out + norm_back(resid, inverse_mlp, grad_normed_mlp * gain_mlp)
    grad_proj = grad_resid.astype(jnp.bfloat16)
    grad_w_proj = trans_times(attended, grad_proj)
    grad_attended = times_trans(grad_proj, back_proj).astype(jnp.bfloat16).reshape(rows, H, HD)
    delta = jnp.transpose(jnp.sum(grad_attended.astype(jnp.float32) * attn_float, axis=-1))

    def backward_step(carried, subrows, offset):
        grad_queries, grad_keyval = carried
        key_count = subrows.shape[0]
        keys_part = subrows[:, :D].reshape(key_count, H, HD)
        values_part = subrows[:, D:].reshape(key_count, H, HD)
        scores = jnp.einsum("qhd,khd->hqk", queries, keys_part, preferred_element_type=jnp.float32)
        allowed = visible(query_pos, query_seg, seg_row, offset, key_count)[None]
        probs = jnp.where(
            allowed, jnp.exp(jnp.where(allowed, scores, masked_fill) - logsum[:, :, None]), 0.0
        )
        grad_probs = jnp.einsum(
            "qhd,khd->hqk", grad_attended, values_part, preferred_element_type=jnp.float32
        )
        grad_scores = (probs * (grad_probs - delta[:, :, None])).astype(jnp.bfloat16)
        grad_queries = grad_queries + jnp.einsum(
            "hqk,khd->qhd", grad_scores, keys_part, preferred_element_type=jnp.float32
        )
        grad_keys = jnp.einsum(
            "hqk,qhd->khd", grad_scores, queries, preferred_element_type=jnp.float32
        )
        grad_values = jnp.einsum(
            "hqk,qhd->khd",
            probs.astype(jnp.bfloat16),
            grad_attended,
            preferred_element_type=jnp.float32,
        )
        combined = jnp.concatenate(
            [grad_keys.reshape(key_count, D), grad_values.reshape(key_count, D)], axis=1
        )
        current = lax.dynamic_slice_in_dim(grad_keyval, offset, key_count, 0)
        grad_keyval = lax.dynamic_update_slice_in_dim(grad_keyval, current + combined, offset, 0)
        return (grad_queries, grad_keyval)

    back_state = (jnp.zeros((rows, H, HD), jnp.float32), jnp.zeros((group_len, 2 * D), jnp.float32))
    grad_queries, grad_keyval = blocked(
        backward_step, back_state, lax.all_gather(keyval, "ctx", axis=0, tiled=True)
    )
    grad_keyval_own = lax.psum_scatter(
        grad_keyval.astype(jnp.bfloat16), "ctx", scatter_dimension=0, tiled=True
    ).astype(jnp.float32)
    grad_dims = jnp.sum(grad_queries * raw_queries, axis=(0, 1))
    grad_query_scale = grad_dims * (scale_base / math.sqrt(HD)) * jax.nn.sigmoid(query_scale)
    grad_project = jnp.concatenate(
        [(grad_queries * dim_scale).reshape(rows, D), grad_keyval_own], axis=1
    ).astype(jnp.bfloat16)
    grad_w_qkv = trans_times(normed, grad_project)
    grad_normed = times_trans(grad_project, back_qkv)
    grad_gain_attn = jnp.sum(grad_normed * inputs * inverse_attn, axis=0)
    grad_tokens = (grad_resid + norm_back(inputs, inverse_attn, grad_normed * gain_attn)).astype(
        jnp.bfloat16
    )
    shard_qkv, shard_proj, shard_in, shard_out = (
        lax.psum_scatter(
            grad_w_qkv.astype(jnp.bfloat16), "wt", scatter_dimension=0, tiled=True
        ).astype(jnp.float32),
        lax.psum_scatter(
            grad_w_proj.astype(jnp.bfloat16), "wt", scatter_dimension=0, tiled=True
        ).astype(jnp.float32),
        lax.psum_scatter(
            grad_w_in.astype(jnp.bfloat16), "wt", scatter_dimension=0, tiled=True
        ).astype(jnp.float32),
        lax.psum_scatter(
            grad_w_out.astype(jnp.bfloat16), "wt", scatter_dimension=0, tiled=True
        ).astype(jnp.float32),
    )
    total_qkv, total_proj, total_in, total_out = (
        lax.psum(shard_qkv.astype(jnp.bfloat16), ("grp", "ctx")).astype(jnp.float32),
        lax.psum(shard_proj.astype(jnp.bfloat16), ("grp", "ctx")).astype(jnp.float32),
        lax.psum(shard_in.astype(jnp.bfloat16), ("grp", "ctx")).astype(jnp.float32),
        lax.psum(shard_out.astype(jnp.bfloat16), ("grp", "ctx")).astype(jnp.float32),
    )
    total_gain_attn, total_gain_mlp, total_scale = lax.psum(
        (grad_gain_attn, grad_gain_mlp, grad_query_scale), ("grp", "ctx", "wt")
    )
    return (
        layer_out[None],
        grad_tokens[None],
        total_qkv,
        total_proj,
        total_in,
        total_out,
        total_gain_attn,
        total_gain_mlp,
        total_scale,
    )


def solution(mesh):
    placed = (
        P(("grp", "wt"), "ctx", None),
        P(("grp", "wt"), None),
        P("wt", None),
        P("wt", None),
        P("wt", None),
        P("wt", None),
        P(),
        P(),
        P(),
        P(("grp", "wt"), "ctx", None),
    )
    return jax.shard_map(
        local,
        mesh=mesh,
        in_specs=placed,
        out_specs=(
            P(("grp", "wt"), "ctx", None),
            P(("grp", "wt"), "ctx", None),
            P("wt", None),
            P("wt", None),
            P("wt", None),
            P("wt", None),
            P(),
            P(),
            P(),
        ),
        check_vma=False,
    )
```

profile of v0, /device:TPU:0, one launch (start us, length us, event | category | flops | bytes accessed | tf_op | source)
XLA Modules:
  0.0 1364.7 jit_solution(8203904737533730321)
XLA Ops:
  9.4 125.2 %all-gather.6.cloned.1.call-done = bf16[1280,3840]{1,0:T(8,128)(2,1)} async-done(((bf16[640,3840]{1,0:T(8,128)(2,1)}), bf16[1280,3840]{1,0:T(8,128)(2,1)}) %all-gather.6.cloned.1.call-update) | async-done | bytes 9830416 | tf_op jit(solution)/shard_map/all_gather | solution.py:69
  156.0 175.5 %all-gather.8.cloned.1.call-done = bf16[2048,2560]{1,0:T(8,128)(2,1)} async-done(((bf16[512,2560]{1,0:T(8,128)(2,1)}), bf16[2048,2560]{1,0:T(8,128)(2,1)}) %all-gather.8.cloned.1.call-update) | async-done | bytes 10485776 | tf_op jit(solution)/shard_map/all_gather | solution.py:108
  331.5 14.6 %copy.34 = bf16[2048,2560]{0,1:T(8,128)(2,1)} copy(bf16[2048,2560]{1,0:T(8,128)(2,1)} %all-gather.8.cloned.1.call-done) | data formatting | bytes 20971520
  346.1 122.1 %while.34 = (s32[]{:T(128)}, f32[16,512]{1,0:T(8,128)S(1)}, f32[16,512]{1,0:T(8,128)S(1)}, f32[512,16,80]{0,2,1:T(8,128)}, s32[2048]{0:T(1024)S(1)}, /*index=5*/...) while((s32[]{:T(128)}, f32[16,512]{1,0:T(8,128)S(1)}, ...), condition=%wide.region_4.5_spmd.clone, body=%wide.region_1.4_spmd.clone.sunk | while | flops 1387185664 | bytes 66340068 | solution.py:54
  356.6 9.2 fusion.115
  365.8 9.7 bitcast_add_fusion.4
  386.8 10.0 fusion.115
  396.7 10.4 bitcast_add_fusion.4
  417.8 9.2 fusion.115
  427.0 10.7 bitcast_add_fusion.4
  448.4 9.2 fusion.115
  457.5 10.4 bitcast_add_fusion.4
  500.7 9.7 broadcast_in_dim.141
  510.4 188.2 %while.35 = (s32[]{:T(128)}, f32[512,16,80]{0,2,1:T(8,128)}, f32[2048,2560]{0,1:T(8,128)}, bf16[2048,2560]{0,1:T(8,128)(2,1)}, s32[2048]{0:T(1024)S(1)}, /*index...) while((s32[]{:T(128)}, f32[512,16,80]{0,2,1:T(8,128)}, ...), condition=%wide.region_9.10_spmd.clone, body=%wide.region_8.9_spmd.clone.sunk | while | flops 3402368512 | bytes 138003792 | solution.py:54
  523.4 11.4 fusion.130
  534.8 9.7 fusion.129
  569.0 11.4 fusion.130
  580.4 9.7 fusion.129
  616.4 11.4 fusion.130
  627.8 9.7 fusion.129
  663.7 11.4 fusion.130
  675.1 9.7 fusion.129
  698.6 12.3 convert_element_type.118
  736.2 151.1 %reduce-scatter.6.cloned.1.call-done = bf16[512,2560]{0,1:T(8,128)(2,1)} async-done(((bf16[2048,2560]{0,1:T(8,128)(2,1)}), bf16[512,2560]{0,1:T(8,128)(2,1)}) %reduce-scatter.6.cloned.1.call-update) | async-done | bytes 2621456 | tf_op jit(solution)/shard_map/reduce_scatter | solution.py:181
  887.3 10.9 convolution_convert_fusion
  898.4 37.5 %reduce-scatter.12.cloned.1.call-done = bf16[640,1280]{1,0:T(8,128)(2,1)} async-done(((bf16[1280,1280]{1,0:T(8,128)(2,1)}), bf16[640,1280]{1,0:T(8,128)(2,1)}) %reduce-scatter.12.cloned.1.call-update) | async-done | bytes 1638416 | tf_op jit(solution)/shard_map/reduce_scatter | solution.py:202
  936.0 47.7 %reduce-scatter.14.cloned.1.call-done = bf16[640,1280]{1,0:T(8,128)(2,1)} async-done(((bf16[1280,1280]{1,0:T(8,128)(2,1)}), bf16[640,1280]{1,0:T(8,128)(2,1)}) %reduce-scatter.14.cloned.1.call-update) | async-done | bytes 1638416 | tf_op jit(solution)/shard_map/reduce_scatter | solution.py:205
  983.7 47.6 %reduce-scatter.10.cloned.1.call-done = bf16[640,1280]{1,0:T(8,128)(2,1)} async-done(((bf16[1280,1280]{1,0:T(8,128)(2,1)}), bf16[640,1280]{1,0:T(8,128)(2,1)}) %reduce-scatter.10.cloned.1.call-update) | async-done | bytes 1638416 | tf_op jit(solution)/shard_map/reduce_scatter | solution.py:199
  1031.3 117.7 %reduce-scatter.8.cloned.1.call-done = bf16[640,3840]{1,0:T(8,128)(2,1)} async-done(((bf16[1280,3840]{1,0:T(8,128)(2,1)}), bf16[640,3840]{1,0:T(8,128)(2,1)}) %reduce-scatter.8.cloned.1.call-update) | async-done | bytes 4915216 | tf_op jit(solution)/shard_map/reduce_scatter | solution.py:196
  1156.6 12.2 fusion.40
  1168.8 41.6 %all-reduce = (f32[1280]{0:T(1024)}, f32[1280]{0:T(1024)}, f32[80]{0:T(128)}) all-reduce(f32[1280]{0:T(1024)S(1)} %get-tuple-element.469, f32[1280]{0:T(1024)S(1)} %copy-done.24, f32[80]{0:T(128)S(1)} %divide_multiply_fusion), channel_id=1, replica_groups=mesh['grp'=4,'ctx'=4,'wt'=2] {'grp','ctx','wt'}, use_global_device_ids=true, to_apply=%region_21.22 | all-reduce | flops 2640 | bytes 21120 | tf_op jit(solution)/shard_map/psum | solution.py:215
  1214.8 131.1 %all-reduce.4.cloned.1.call-done = (bf16[640,3840]{1,0:T(8,128)(2,1)}, bf16[640,1280]{1,0:T(8,128)(2,1)}, bf16[640,1280]{1,0:T(8,128)(2,1)}, bf16[640,1280]{1,0:T(8,128)(2,1)}) async-done(((bf16[640,3840]{1,0:T(8,128)(2,1)}, bf16[640,1280]{1,0:T(8,128)(2,1)}, bf16[640,1280]{1,0:T(8,128)(2,1)}, bf16[640,1280]{1,0:T(8,128)(2,1)}), (bf16[640,3840]{1,0:T(8,128)(2,1)}, bf16[640,1280]{1,0:T(8,128)(2,1)}, ...) | async-done | bytes 9830416 | tf_op jit(solution)/shard_map/psum | solution.py:210
  (222 shorter events, 251.4 us)
Async XLA Ops:
  7.2 127.5 %copy-start.19 = (f32[1280]{0:T(1024)S(1)}, f32[1280]{0:T(1024)}, u32[]{:S(2)}) copy-start(f32[1280]{0:T(1024)} %param.20) | copy-start | bytes 15364
  7.2 127.4 %all-gather.6.cloned.1.call-start = ((), (), s32[]{:S(2)}) async-start(), calls=%async_computation.5 | async-start | bytes 14745600 | tf_op jit(solution)/shard_map/all_gather | solution.py:69
  7.9 323.5 %all-gather.8.cloned.1.call-start = ((), (), s32[]{:S(2)}) async-start(), calls=%async_computation.6 | async-start | bytes 13107200 | tf_op jit(solution)/shard_map/all_gather | solution.py:108
  9.4 132.9 %copy-start.22 = (f32[512]{0:T(512)}, f32[512]{0:T(512)S(1)}, u32[]{:S(2)}) copy-start(f32[512]{0:T(512)S(1)} %get-tuple-element.537) | copy-start | bytes 6148
  147.4 324.1 %all-gather.10.cloned.1.call-start = ((), (), s32[]{:S(2)}) async-start(), calls=%async_computation.7 | async-start | bytes 4915200 | tf_op jit(solution)/shard_map/all_gather | solution.py:70
  148.1 329.2 %all-gather.12.cloned.1.call-start = ((), (), s32[]{:S(2)}) async-start(), calls=%async_computation.8 | async-start | bytes 4915200 | tf_op jit(solution)/shard_map/all_gather | solution.py:71
  148.7 334.9 %all-gather.14.cloned.1.call-start = ((), (), s32[]{:S(2)}) async-start(), calls=%async_computation.9 | async-start | bytes 4915200 | tf_op jit(solution)/shard_map/all_gather | solution.py:72
  149.3 738.0 %reduce-scatter.6.cloned.1.call-start = ((), (), s32[]{:S(2)}) async-start(), calls=%async_computation.10 | async-start | bytes 13107200 | tf_op jit(solution)/shard_map/reduce_scatter | solution.py:181
  149.6 3.9 copy-start.29
  471.5 5.9 copy-start.25
  477.3 14.2 %copy-start.27 = (f32[512]{0:T(512)}, f32[512]{0:T(512)S(1)}, u32[]{:S(2)}) copy-start(f32[512]{0:T(512)S(1)} %get-tuple-element.539) | copy-start | bytes 6148
  477.3 6.3 copy-start.16
  483.6 5.1 copy-start.6
  483.6 5.1 copy-start.31
  550.2 6.2 copy-start.12
  597.5 6.3 copy-start.12
  644.9 6.2 copy-start.12
  692.2 6.2 copy-start.12
  710.9 225.1 %reduce-scatter.12.cloned.1.call-start = ((), (), s32[]{:S(2)}) async-start(), calls=%async_computation.13 | async-start | bytes 4915200 | tf_op jit(solution)/shard_map/reduce_scatter | solution.py:202
  717.6 266.1 %reduce-scatter.14.cloned.1.call-start = ((), (), s32[]{:S(2)}) async-start(), calls=%async_computation.14 | async-start | bytes 4915200 | tf_op jit(solution)/shard_map/reduce_scatter | solution.py:205
  724.4 307.0 %reduce-scatter.10.cloned.1.call-start = ((), (), s32[]{:S(2)}) async-start(), calls=%async_computation.12 | async-start | bytes 4915200 | tf_op jit(solution)/shard_map/reduce_scatter | solution.py:199
  731.0 418.0 %reduce-scatter.8.cloned.1.call-start = ((), (), s32[]{:S(2)}) async-start(), calls=%async_computation.11 | async-start | bytes 14745600 | tf_op jit(solution)/shard_map/reduce_scatter | solution.py:196
  732.7 154.6 %copy-start.20 = (f32[1280]{0:T(1024)S(1)}, f32[1280]{0:T(1024)}, u32[]{:S(2)}) copy-start(f32[1280]{0:T(1024)} %param.20) | copy-start | bytes 15364
  732.7 154.6 %copy-start.23 = (f32[512]{0:T(512)S(1)}, f32[512]{0:T(512)}, u32[]{:S(2)}) copy-start(f32[512]{0:T(512)} %copy-done.22) | copy-start | bytes 6148
  898.2 447.7 %all-reduce.4.cloned.1.call-start = ((), (), s32[]{:S(2)}) async-start(), calls=%async_computation.15 | async-start | bytes 19660800 | tf_op jit(solution)/shard_map/psum | solution.py:210
  1149.7 6.9 copy-start.4
  1149.7 6.9 copy-start.15
  1149.7 6.9 copy-start.32
  1156.6 12.2 copy-start.24
  1156.6 53.8 %copy-start.21 = (f32[512]{0:T(512)S(1)}, f32[512]{0:T(512)}, u32[]{:S(2)}) copy-start(f32[512]{0:T(512)} %get-tuple-element.536) | copy-start | bytes 6148
  1345.9 7.5 slice-start.1
  1349.4 3.9 slice-start.2
  (27 other events, 53.3 us)
Sparse Core Ops, SparseCore 0:
  9.6 125.0 all-gather.5
  147.5 183.9 all-gather.7
  333.0 44.5 all-gather.9
  379.0 46.4 all-gather.11
  426.9 46.3 all-gather.13
  711.0 176.2 reduce-scatter.5
  890.1 45.8 reduce-scatter.11
  938.9 44.7 reduce-scatter.13
  986.5 44.7 reduce-scatter.9
  1034.2 114.7 reduce-scatter.7
  1153.0 192.8 all-reduce.3
where the time goes:
time: 1370 us; the launch traced here: 1360 us
  waiting for transfers between devices  836 us (61%)
  matrix products  296 us (22%)
  other arithmetic  108 us (8%)
  local copies, waits for them, and re-layouts  67.2 us (5%)
  blocking collectives  41.6 us (3%)
  between operations  14.5 us (1%)
    all_gather x1, waiting for transfers between devices, local(): lax.all_gather(keyval, 'ctx', axis=0, tiled=True)  175 us
    reduce_scatter x1, waiting for transfers between devices, local(): lax.psum_scatter(grad_keyval.astype(jnp.bfloat16), 'ctx', scatter_dimensi...  151 us
    psum x1, waiting for transfers between devices, local(): lax.psum(shard_qkv.astype(jnp.bfloat16), ('grp', 'ctx')).astype(jnp.float32)  131 us
    all_gather x1, waiting for transfers between devices, local(): lax.all_gather(w_qkv, 'wt', axis=0, tiled=True)  125 us
    reduce_scatter x1, waiting for transfers between devices, local(): lax.psum_scatter(grad_w_qkv.astype(jnp.bfloat16), 'wt', scatter_dimension...  118 us
    reduce_scatter x1, waiting for transfers between devices, local(): lax.psum_scatter(grad_w_out.astype(jnp.bfloat16), 'wt', scatter_dimension...  47.7 us
    reduce_scatter x1, waiting for transfers between devices, local(): lax.psum_scatter(grad_w_proj.astype(jnp.bfloat16), 'wt', scatter_dimensio...  47.6 us
    dot_general x4, matrix products, backward_step(): jnp.einsum('hqk,qhd->khd', probs.astype(jnp.bfloat16), grad_attended, pre...  45.8 us
  transfers between devices with their start and end apart: 11, of which 8 were waited for; matrix products, arithmetic and copies ran while one was open for 15% of the time, Pallas kernels for 0%

commit v1 on v0

--- a/solution.py
+++ b/solution.py
@@ -213,7 +213,7 @@
         lax.psum(shard_out.astype(jnp.bfloat16), ("grp", "ctx")).astype(jnp.float32),
     )
     total_gain_attn, total_gain_mlp, total_scale = lax.psum(
-        (grad_gain_attn, grad_gain_mlp, grad_query_scale), ("grp", "ctx", "wt")
+        lax.psum((grad_gain_attn, grad_gain_mlp, grad_query_scale), ("ctx", "wt")), "grp"
     )
     return (
         layer_out[None],

time: 1370 us -> 1370 us (level)
    psum x1 -> x2, blocking collectives: 41.6 us -> 49.2 us  [the longest x1 37.6 us: local(): lax.psum((grad_gain_attn, grad_gain_mlp, grad_query_scale), ('ctx', 'wt'))]
where the time goes in v1:
time: 1370 us; the launch traced here: 1360 us
  waiting for transfers between devices  828 us (60%)
  matrix products  296 us (22%)
  other arithmetic  108 us (8%)
  local copies, waits for them, and re-layouts  67.2 us (5%)
  blocking collectives  49.2 us (4%)
  between operations  14.5 us (1%)
    all_gather x1, waiting for transfers between devices, local(): lax.all_gather(keyval, 'ctx', axis=0, tiled=True)  175 us
    reduce_scatter x1, waiting for transfers between devices, local(): lax.psum_scatter(grad_keyval.astype(jnp.bfloat16), 'ctx', scatter_dimensi...  151 us
    all_gather x1, waiting for transfers between devices, local(): lax.all_gather(w_qkv, 'wt', axis=0, tiled=True)  125 us
    psum x1, waiting for transfers between devices, local(): lax.psum(shard_qkv.astype(jnp.bfloat16), ('grp', 'ctx')).astype(jnp.float32)  123 us
    reduce_scatter x1, waiting for transfers between devices, local(): lax.psum_scatter(grad_w_qkv.astype(jnp.bfloat16), 'wt', scatter_dimension...  118 us
    reduce_scatter x1, waiting for transfers between devices, local(): lax.psum_scatter(grad_w_out.astype(jnp.bfloat16), 'wt', scatter_dimension...  47.7 us
    reduce_scatter x1, waiting for transfers between devices, local(): lax.psum_scatter(grad_w_proj.astype(jnp.bfloat16), 'wt', scatter_dimensio...  47.6 us
    dot_general x4, matrix products, backward_step(): jnp.einsum('hqk,qhd->khd', probs.astype(jnp.bfloat16), grad_attended, pre...  45.8 us
  transfers between devices with their start and end apart: 11, of which 8 were waited for; matrix products, arithmetic and copies ran while one was open for 15% of the time, Pallas kernels for 0%

profile of v1, /device:TPU:0, one launch (start us, length us, event | category | flops | bytes accessed | tf_op | source)
XLA Modules:
  0.0 1364.5 jit_solution(5558013914821766928)
XLA Ops:
  9.4 125.2 %all-gather.6.cloned.1.call-done = bf16[1280,3840]{1,0:T(8,128)(2,1)} async-done(((bf16[640,3840]{1,0:T(8,128)(2,1)}), bf16[1280,3840]{1,0:T(8,128)(2,1)}) %all-gather.6.cloned.1.call-update) | async-done | bytes 9830416 | tf_op jit(solution)/shard_map/all_gather | solution.py:69
  156.0 175.5 %all-gather.8.cloned.1.call-done = bf16[2048,2560]{1,0:T(8,128)(2,1)} async-done(((bf16[512,2560]{1,0:T(8,128)(2,1)}), bf16[2048,2560]{1,0:T(8,128)(2,1)}) %all-gather.8.cloned.1.call-update) | async-done | bytes 10485776 | tf_op jit(solution)/shard_map/all_gather | solution.py:108
  331.5 14.7 %copy.34 = bf16[2048,2560]{0,1:T(8,128)(2,1)} copy(bf16[2048,2560]{1,0:T(8,128)(2,1)} %all-gather.8.cloned.1.call-done) | data formatting | bytes 20971520
  346.1 122.2 %while.34 = (s32[]{:T(128)}, f32[16,512]{1,0:T(8,128)S(1)}, f32[16,512]{1,0:T(8,128)S(1)}, f32[512,16,80]{0,2,1:T(8,128)}, s32[2048]{0:T(1024)S(1)}, /*index=5*/...) while((s32[]{:T(128)}, f32[16,512]{1,0:T(8,128)S(1)}, ...), condition=%wide.region_4.5_spmd.clone, body=%wide.region_1.4_spmd.clone.sunk | while | flops 1387185664 | bytes 66340068 | solution.py:54
  356.7 9.2 fusion.115
  365.9 9.7 bitcast_add_fusion.4
  386.9 9.9 fusion.115
  396.8 10.4 bitcast_add_fusion.4
  417.9 9.2 fusion.115
  427.1 10.8 bitcast_add_fusion.4
  457.6 10.4 bitcast_add_fusion.4
  500.8 9.7 broadcast_in_dim.141
  510.5 188.1 %while.35 = (s32[]{:T(128)}, f32[512,16,80]{0,2,1:T(8,128)}, f32[2048,2560]{0,1:T(8,128)}, bf16[2048,2560]{0,1:T(8,128)(2,1)}, s32[2048]{0:T(1024)S(1)}, /*index...) while((s32[]{:T(128)}, f32[512,16,80]{0,2,1:T(8,128)}, ...), condition=%wide.region_9.10_spmd.clone, body=%wide.region_8.9_spmd.clone.sunk | while | flops 3402368512 | bytes 138003792 | solution.py:54
  523.5 11.4 fusion.130
  534.9 9.7 fusion.129
  569.1 11.4 fusion.130
  580.5 9.7 fusion.129
  616.4 11.4 fusion.130
  627.8 9.7 fusion.129
  663.7 11.4 fusion.130
  675.2 9.7 fusion.129
  698.6 12.3 convert_element_type.118
  736.3 151.1 %reduce-scatter.6.cloned.1.call-done = bf16[512,2560]{0,1:T(8,128)(2,1)} async-done(((bf16[2048,2560]{0,1:T(8,128)(2,1)}), bf16[512,2560]{0,1:T(8,128)(2,1)}) %reduce-scatter.6.cloned.1.call-update) | async-done | bytes 2621456 | tf_op jit(solution)/shard_map/reduce_scatter | solution.py:181
  887.4 10.9 convolution_convert_fusion
  898.5 37.5 %reduce-scatter.12.cloned.1.call-done = bf16[640,1280]{1,0:T(8,128)(2,1)} async-done(((bf16[1280,1280]{1,0:T(8,128)(2,1)}), bf16[640,1280]{1,0:T(8,128)(2,1)}) %reduce-scatter.12.cloned.1.call-update) | async-done | bytes 1638416 | tf_op jit(solution)/shard_map/reduce_scatter | solution.py:202
  936.0 47.7 %reduce-scatter.14.cloned.1.call-done = bf16[640,1280]{1,0:T(8,128)(2,1)} async-done(((bf16[1280,1280]{1,0:T(8,128)(2,1)}), bf16[640,1280]{1,0:T(8,128)(2,1)}) %reduce-scatter.14.cloned.1.call-update) | async-done | bytes 1638416 | tf_op jit(solution)/shard_map/reduce_scatter | solution.py:205
  983.8 47.6 %reduce-scatter.10.cloned.1.call-done = bf16[640,1280]{1,0:T(8,128)(2,1)} async-done(((bf16[1280,1280]{1,0:T(8,128)(2,1)}), bf16[640,1280]{1,0:T(8,128)(2,1)}) %reduce-scatter.10.cloned.1.call-update) | async-done | bytes 1638416 | tf_op jit(solution)/shard_map/reduce_scatter | solution.py:199
  1031.4 117.7 %reduce-scatter.8.cloned.1.call-done = bf16[640,3840]{1,0:T(8,128)(2,1)} async-done(((bf16[1280,3840]{1,0:T(8,128)(2,1)}), bf16[640,3840]{1,0:T(8,128)(2,1)}) %reduce-scatter.8.cloned.1.call-update) | async-done | bytes 4915216 | tf_op jit(solution)/shard_map/reduce_scatter | solution.py:196
  1156.7 12.2 fusion.40
  1168.9 37.6 %all-reduce = (f32[1280]{0:T(1024)S(1)}, f32[1280]{0:T(1024)S(1)}, f32[80]{0:T(128)S(1)}) all-reduce(f32[1280]{0:T(1024)S(1)} %get-tuple-element.469, f32[1280]{0:T(1024)S(1)} %copy-done.24, f32[80]{0:T(128)S(1)} %divide_multiply_fusion), channel_id=1, replica_groups=mesh['grp'=4,'ctx'=4,'wt'=2] {'ctx','wt'}, use_global_device_ids=true, to_apply=%region_21.22 | all-reduce | flops 2640 | bytes 21120 | tf_op jit(solution)/shard_map/psum | solution.py:216
  1206.4 11.6 all-reduce.1
  1222.4 123.2 %all-reduce.5.cloned.1.call-done = (bf16[640,3840]{1,0:T(8,128)(2,1)}, bf16[640,1280]{1,0:T(8,128)(2,1)}, bf16[640,1280]{1,0:T(8,128)(2,1)}, bf16[640,1280]{1,0:T(8,128)(2,1)}) async-done(((bf16[640,3840]{1,0:T(8,128)(2,1)}, bf16[640,1280]{1,0:T(8,128)(2,1)}, bf16[640,1280]{1,0:T(8,128)(2,1)}, bf16[640,1280]{1,0:T(8,128)(2,1)}), (bf16[640,3840]{1,0:T(8,128)(2,1)}, bf16[640,1280]{1,0:T(8,128)(2,1)}, ...) | async-done | bytes 9830416 | tf_op jit(solution)/shard_map/psum | solution.py:210
  (223 shorter events, 260.5 us)
Async XLA Ops:
  7.2 127.5 %copy-start.19 = (f32[1280]{0:T(1024)S(1)}, f32[1280]{0:T(1024)}, u32[]{:S(2)}) copy-start(f32[1280]{0:T(1024)} %param.20) | copy-start | bytes 15364
  7.2 127.4 %all-gather.6.cloned.1.call-start = ((), (), s32[]{:S(2)}) async-start(), calls=%async_computation.5 | async-start | bytes 14745600 | tf_op jit(solution)/shard_map/all_gather | solution.py:69
  7.9 323.5 %all-gather.8.cloned.1.call-start = ((), (), s32[]{:S(2)}) async-start(), calls=%async_computation.6 | async-start | bytes 13107200 | tf_op jit(solution)/shard_map/all_gather | solution.py:108
  9.4 132.9 %copy-start.22 = (f32[512]{0:T(512)}, f32[512]{0:T(512)S(1)}, u32[]{:S(2)}) copy-start(f32[512]{0:T(512)S(1)} %get-tuple-element.540) | copy-start | bytes 6148
  147.4 324.2 %all-gather.10.cloned.1.call-start = ((), (), s32[]{:S(2)}) async-start(), calls=%async_computation.7 | async-start | bytes 4915200 | tf_op jit(solution)/shard_map/all_gather | solution.py:70
  148.1 329.3 %all-gather.12.cloned.1.call-start = ((), (), s32[]{:S(2)}) async-start(), calls=%async_computation.8 | async-start | bytes 4915200 | tf_op jit(solution)/shard_map/all_gather | solution.py:71
  148.7 335.0 %all-gather.14.cloned.1.call-start = ((), (), s32[]{:S(2)}) async-start(), calls=%async_computation.9 | async-start | bytes 4915200 | tf_op jit(solution)/shard_map/all_gather | solution.py:72
  149.3 738.1 %reduce-scatter.6.cloned.1.call-start = ((), (), s32[]{:S(2)}) async-start(), calls=%async_computation.10 | async-start | bytes 13107200 | tf_op jit(solution)/shard_map/reduce_scatter | solution.py:181
  149.6 3.9 copy-start.29
  471.6 5.9 copy-start.25
  477.4 14.2 %copy-start.27 = (f32[512]{0:T(512)}, f32[512]{0:T(512)S(1)}, u32[]{:S(2)}) copy-start(f32[512]{0:T(512)S(1)} %get-tuple-element.542) | copy-start | bytes 6148
  477.5 6.3 copy-start.16
  483.8 5.1 copy-start.8
  483.8 5.1 copy-start.31
  550.3 6.2 copy-start.12
  597.6 6.2 copy-start.12
  644.9 6.2 copy-start.12
  692.2 6.3 copy-start.12
  710.9 225.1 %reduce-scatter.12.cloned.1.call-start = ((), (), s32[]{:S(2)}) async-start(), calls=%async_computation.13 | async-start | bytes 4915200 | tf_op jit(solution)/shard_map/reduce_scatter | solution.py:202
  717.7 266.1 %reduce-scatter.14.cloned.1.call-start = ((), (), s32[]{:S(2)}) async-start(), calls=%async_computation.14 | async-start | bytes 4915200 | tf_op jit(solution)/shard_map/reduce_scatter | solution.py:205
  724.4 307.0 %reduce-scatter.10.cloned.1.call-start = ((), (), s32[]{:S(2)}) async-start(), calls=%async_computation.12 | async-start | bytes 4915200 | tf_op jit(solution)/shard_map/reduce_scatter | solution.py:199
  731.1 418.0 %reduce-scatter.8.cloned.1.call-start = ((), (), s32[]{:S(2)}) async-start(), calls=%async_computation.11 | async-start | bytes 14745600 | tf_op jit(solution)/shard_map/reduce_scatter | solution.py:196
  732.8 154.6 %copy-start.20 = (f32[1280]{0:T(1024)S(1)}, f32[1280]{0:T(1024)}, u32[]{:S(2)}) copy-start(f32[1280]{0:T(1024)} %param.20) | copy-start | bytes 15364
  732.8 154.6 %copy-start.23 = (f32[512]{0:T(512)S(1)}, f32[512]{0:T(512)}, u32[]{:S(2)}) copy-start(f32[512]{0:T(512)} %copy-done.22) | copy-start | bytes 6148
  898.3 447.4 %all-reduce.5.cloned.1.call-start = ((), (), s32[]{:S(2)}) async-start(), calls=%async_computation.15 | async-start | bytes 19660800 | tf_op jit(solution)/shard_map/psum | solution.py:210
  1149.8 6.9 copy-start.4
  1149.8 6.9 copy-start.15
  1149.8 6.9 copy-start.32
  1156.7 12.2 copy-start.24
  1156.7 61.4 %copy-start.21 = (f32[512]{0:T(512)S(1)}, f32[512]{0:T(512)}, u32[]{:S(2)}) copy-start(f32[512]{0:T(512)} %get-tuple-element.539) | copy-start | bytes 6148
  1345.6 7.5 slice-start.1
  1349.2 3.9 slice-start.2
  (27 other events, 53.3 us)
Sparse Core Ops, SparseCore 0:
  9.6 125.0 all-gather.5
  147.5 183.9 all-gather.7
  333.0 44.5 all-gather.9
  379.0 46.4 all-gather.11
  426.9 46.4 all-gather.13
  711.1 176.2 reduce-scatter.5
  890.2 45.8 reduce-scatter.11
  939.0 44.7 reduce-scatter.13
  986.6 44.7 reduce-scatter.9
  1034.3 114.7 reduce-scatter.7
  1153.1 192.5 all-reduce.4
